TPU v7x, 32 devices: a whole 2x2x4 slice. The times are simulated.
32 devices in a mesh: groups: 2 (over y), section: 2 (over x), shard: 8 (over z, core).
Axes of the slice: x: 2, y: 2, z: 4, core: 2. Of those that a mesh axis runs over, the one named last changes fastest.
Arguments:
- embed: bfloat16 [1024, 8192], P('groups', 'shard'), parts along dimension 0, may hold values from -6 to 6
- gains: float32 [4, 8192], P('section', 'shard'), may hold values from 0.25 to 1.75
- theta: float32 [4, 8, 2, 64, 8192], P('section', 'groups', None, None, 'shard'), parts along dimension 1, may hold values from -6 to 6
- iterate: float32 [4, 8, 2, 64, 8192], P('section', 'groups', None, None, 'shard'), parts along dimension 1, may hold values from -6 to 6
- residual: float32 [4, 8, 2, 64, 8192], P('section', 'groups', None, None, 'shard'), parts along dimension 1, may hold values from -6 to 6
- direction: float32 [4, 8, 2, 64, 8192], P('section', 'groups', None, None, 'shard'), parts along dimension 1, may hold values from -6 to 6
- token_task: int32 [1024], P('groups'), parts along dimension 0, may hold values from 0 to 3, never falling along the last dimension, each value on 1 to 256 neighbouring positions
- loss_mask: int32 [1024], P('groups'), parts along dimension 0, may hold values 0 or 1
Outputs:
- new_iterate: float32 [4, 8, 2, 64, 8192], P('section', 'groups', None, None, 'shard'), parts along dimension 1
- updated_residual_stream: float32 [4, 8, 2, 64, 8192], P('section', 'groups', None, None, 'shard'), parts along dimension 1
- new_direction: float32 [4, 8, 2, 64, 8192], P('section', 'groups', None, None, 'shard'), parts along dimension 1
There are 2 independent parts, one for each index of `groups`. A program takes and returns all parts, laid end to end along the dimension named above; an argument that names none is the same for every part. Nothing has to cross between parts.
Inputs may be any that keep to these rules, and one draw needn't show every extreme that they name: `token_task`: tokens of one task stand together, tasks in increasing order; each task has 1 to 256 tokens and one has exactly 256.
All inputs are finite; a program needn't handle non-finite values.
Results may differ from a plain program's by a relative error of at most 0.0003.
Values sent between devices are 32-bit elements; how exact they have to be, the bound alone decides.
A program may use at most 128 MiB of HBM per device.

v0:
```python
import jax
import jax.numpy as jnp
from jax import lax
from jax.sharding import PartitionSpec as P

D = 8192
ADAPTER_RANK = 64
MICRO = 2
EPSILON = 1e-05
ADAPTER_SCALE = 0.5
DAMPING_FACTOR = 0.5
HIGH = lax.Precision.HIGHEST


def shifted(value, axis, steps):
    count = lax.axis_size(axis)
    initial, last = (max(0, -steps), min(count, count - steps))
    return lax.ppermute(value, axis, [(source, source + steps) for source in range(initial, last)])


def pick_down(values, mats, onehot):
    expanded = jnp.einsum("td,krd->tkr", values, mats, precision=HIGH)
    return jnp.sum(expanded * onehot[:, :, None], axis=1)


def apply_up_projection(lowrank, mats, onehot):
    picked = onehot[:, :, None] * lowrank[:, None, :]
    return jnp.einsum("tkr,krd->td", picked, mats, precision=HIGH)


def task_outer(lowrank, values, onehot):
    picked = onehot[:, :, None] * lowrank[:, None, :]
    return jnp.einsum("tkr,td->krd", picked, values, precision=HIGH)


def keep_rows(store, value, layer_index, row_start, active):
    index = (jnp.int32(layer_index), row_start) + tuple((jnp.int32(0) for extra in value.shape[1:]))
    sizes = (1,) + value.shape
    previous = lax.dynamic_slice(store, index, sizes)[0]
    fresh = jnp.where(active, value, previous)
    return lax.dynamic_update_slice(store, fresh[None], index)


def layer_forward(hidden, moving, onehot, parameters, slope, gain_vector):
    down_scale = D ** (-0.5)
    up_projection_scale = ADAPTER_SCALE * ADAPTER_RANK ** (-0.5)
    scaled = hidden * gain_vector
    squares, products = lax.psum(
        (jnp.sum(hidden * hidden, axis=-1), jnp.sum(hidden * moving, axis=-1)), "shard"
    )
    recip = 1.0 / jnp.sqrt(squares / D + EPSILON)
    drift = -(recip**3) * products / D
    normed = scaled * recip[:, None]
    normed_move = gain_vector * (moving * recip[:, None] + hidden * drift[:, None])
    lowrank, lowmove = lax.psum(
        (
            pick_down(normed, parameters[:, 0], onehot) * down_scale,
            (
                pick_down(normed_move, parameters[:, 0], onehot)
                + pick_down(normed, slope[:, 0], onehot)
            )
            * down_scale,
        ),
        "shard",
    )
    result = hidden + up_projection_scale * apply_up_projection(lowrank, parameters[:, 1], onehot)
    result_move = moving + up_projection_scale * (
        apply_up_projection(lowmove, parameters[:, 1], onehot)
        + apply_up_projection(lowrank, slope[:, 1], onehot)
    )
    return (result, result_move, recip, lowrank)


def layer_backward(cotangent, hidden, recip, lowrank, onehot, parameters, gain_vector):
    down_scale = D ** (-0.5)
    up_projection_scale = ADAPTER_SCALE * ADAPTER_RANK ** (-0.5)
    grad_up = up_projection_scale * task_outer(lowrank, cotangent, onehot)
    partial_cot = up_projection_scale * pick_down(cotangent, parameters[:, 1], onehot)
    low_cot = lax.psum(partial_cot, "shard")
    normed = hidden * gain_vector * recip[:, None]
    grad_down = down_scale * task_outer(low_cot, normed, onehot)
    cot_norm = down_scale * apply_up_projection(low_cot, parameters[:, 0], onehot)
    row_total = lax.psum(jnp.sum(cot_norm * gain_vector * hidden, axis=-1), "shard")
    cot_input = (
        cotangent
        + gain_vector * cot_norm * recip[:, None]
        - (recip**3 * row_total / D)[:, None] * hidden
    )
    return (cot_input, jnp.stack([grad_down, grad_up], axis=1))


def body(embed, gains, theta, iterate, residual, direction, token_task, loss_mask):
    squared_old = lax.psum(jnp.sum(residual * residual), ("section", "shard"))
    section_index = lax.axis_index("section")
    sections = lax.axis_size("section")
    layers_here = theta.shape[0]
    tokens = embed.shape[0]
    width_here = embed.shape[1]
    lowrank_width = theta.shape[3]
    pieces = MICRO
    row_count = tokens // pieces
    onehot = (token_task[:, None] == jnp.arange(theta.shape[1], dtype=jnp.int32)[None, :]).astype(
        jnp.float32
    )
    weights = loss_mask.astype(jnp.float32)
    embedded = embed.astype(jnp.float32)
    saved_hidden = jnp.zeros((layers_here, tokens, width_here), jnp.float32)
    saved_recip = jnp.zeros((layers_here, tokens), jnp.float32)
    saved_low = jnp.zeros((layers_here, tokens, lowrank_width), jnp.float32)
    final_move = jnp.zeros((1, tokens, width_here), jnp.float32)
    incoming = jnp.zeros((row_count, width_here), jnp.float32)
    incoming_move = jnp.zeros((row_count, width_here), jnp.float32)
    for momentum_buffer in range(pieces + sections - 1):
        piece_index = momentum_buffer - section_index
        active = (piece_index >= 0) & (piece_index < pieces)
        row_start = jnp.clip(piece_index, 0, pieces - 1) * row_count
        first_rows = lax.dynamic_slice_in_dim(embedded, row_start, row_count, 0)
        hidden = jnp.where(section_index == 0, first_rows, incoming)
        moving = jnp.where(section_index == 0, jnp.zeros_like(incoming_move), incoming_move)
        onehot_rows = lax.dynamic_slice_in_dim(onehot, row_start, row_count, 0)
        for layer_index in range(layers_here):
            saved_hidden = keep_rows(saved_hidden, hidden, layer_index, row_start, active)
            hidden, moving, recip, lowrank = layer_forward(
                hidden,
                moving,
                onehot_rows,
                theta[layer_index],
                direction[layer_index],
                gains[layer_index],
            )
            saved_recip = keep_rows(saved_recip, recip, layer_index, row_start, active)
            saved_low = keep_rows(saved_low, lowrank, layer_index, row_start, active)
        final_move = keep_rows(final_move, moving, 0, row_start, active)
        incoming, incoming_move = shifted((hidden, moving), "section", 1)
    cot_output = final_move[0] * weights[:, None]
    gradient = jnp.zeros_like(theta)
    incoming_cot = jnp.zeros((row_count, width_here), jnp.float32)
    for momentum_buffer in range(pieces + sections - 1):
        piece_index = momentum_buffer - (sections - 1 - section_index)
        active = (piece_index >= 0) & (piece_index < pieces)
        row_start = jnp.clip(piece_index, 0, pieces - 1) * row_count
        last_rows = lax.dynamic_slice_in_dim(cot_output, row_start, row_count, 0)
        cotangent = jnp.where(section_index == sections - 1, last_rows, incoming_cot)
        onehot_rows = lax.dynamic_slice_in_dim(onehot, row_start, row_count, 0)
        for layer_index in reversed(range(layers_here)):
            hidden = lax.dynamic_slice_in_dim(saved_hidden[layer_index], row_start, row_count, 0)
            recip = lax.dynamic_slice_in_dim(saved_recip[layer_index], row_start, row_count, 0)
            lowrank = lax.dynamic_slice_in_dim(saved_low[layer_index], row_start, row_count, 0)
            cotangent, layer_grad = layer_backward(
                cotangent,
                hidden,
                recip,
                lowrank,
                onehot_rows,
                theta[layer_index],
                gains[layer_index],
            )
            gradient = gradient.at[layer_index].add(jnp.where(active, layer_grad, 0.0))
        incoming_cot = shifted(cotangent, "section", -1)
    product = gradient + DAMPING_FACTOR * direction
    curvature = lax.psum(jnp.sum(direction * product), ("section", "shard"))
    alpha = squared_old / curvature
    new_iterate = iterate + alpha * direction
    updated_residual_stream = residual - alpha * product
    squared_new = lax.psum(
        jnp.sum(updated_residual_stream * updated_residual_stream), ("section", "shard")
    )
    new_direction = updated_residual_stream + squared_new / squared_old * direction
    return (new_iterate, updated_residual_stream, new_direction)


def solution(mesh):
    return jax.shard_map(
        body,
        mesh=mesh,
        in_specs=(
            P("groups", "shard"),
            P("section", "shard"),
            P("section", "groups", None, None, "shard"),
            P("section", "groups", None, None, "shard"),
            P("section", "groups", None, None, "shard"),
            P("section", "groups", None, None, "shard"),
            P("groups"),
            P("groups"),
        ),
        out_specs=(
            P("section", "groups", None, None, "shard"),
            P("section", "groups", None, None, "shard"),
            P("section", "groups", None, None, "shard"),
        ),
        check_vma=False,
    )
```

profile of v0, /device:TPU:0, one launch (start us, length us, event | category | flops | bytes accessed | tf_op | source)
XLA Modules:
  0.0 1198.5 jit_solution(992745657408571423)
XLA Ops:
  19.2 18.1 %all-reduce.6 = (f32[256]{0:T(256)S(1)}, f32[256]{0:T(256)S(1)}) all-reduce(f32[256]{0:T(256)S(1)} %get-tuple-element.79, f32[256]{0:T(256)S(1)} %get-tuple-element.78), channel_id=1, replica_groups=mesh['groups'=2,'section'=2,'shard'=8] {'shard'}, use_global_device_ids=true, to_apply=%region_3.4 | all-reduce | flops 512 | bytes 4096 | tf_op jit(solution)/shard_map/psum | solution.py:48
  54.5 42.4 %all-reduce.48.cloned.1.call-done = (f32[256,64]{0,1:T(8,128)}, f32[256,64]{0,1:T(8,128)}) async-done(((f32[256,64]{0,1:T(8,128)}, f32[256,64]{0,1:T(8,128)}), (f32[256,64]{0,1:T(8,128)}, f32[256,64]{0,1:T(8,128)})) %all-reduce.48.cloned.1.call-update) | async-done | bytes 131088 | tf_op jit(solution)/shard_map/psum | solution.py:55
  102.3 13.9 %all-reduce.5 = (f32[256]{0:T(256)S(1)}, f32[256]{0:T(256)S(1)}) all-reduce(f32[256]{0:T(256)S(1)} %get-tuple-element.89, f32[256]{0:T(256)S(1)} %get-tuple-element.88), channel_id=1, replica_groups=mesh['groups'=2,'section'=2,'shard'=8] {'shard'}, use_global_device_ids=true, to_apply=%region_12.13 | all-reduce | flops 512 | bytes 4096 | tf_op jit(solution)/shard_map/psum | solution.py:48
  123.9 52.4 %all-reduce.46.cloned.1.call-done = (f32[256,64]{0,1:T(8,128)}, f32[256,64]{0,1:T(8,128)}) async-done(((f32[256,64]{0,1:T(8,128)}, f32[256,64]{0,1:T(8,128)}), (f32[256,64]{0,1:T(8,128)}, f32[256,64]{0,1:T(8,128)})) %all-reduce.46.cloned.1.call-update) | async-done | bytes 131088 | tf_op jit(solution)/shard_map/psum | solution.py:55
  189.0 17.4 %collective-permute-done.1 = f32[256,1024]{1,0:T(8,128)S(1)} collective-permute-done((f32[256,1024]{1,0:T(8,128)S(1)}, f32[256,1024]{1,0:T(8,128)S(1)}, u32[]{:S(2)}, u32[]{:S(2)}) %collective-permute-start.1) | collective-permute-done | bytes 1048608 | tf_op jit(solution)/shard_map/ppermute | solution.py:18
  207.7 18.4 %collective-permute-done = f32[256,1024]{1,0:T(8,128)S(1)} collective-permute-done((f32[256,1024]{1,0:T(8,128)S(1)}, f32[256,1024]{1,0:T(8,128)S(1)}, u32[]{:S(2)}, u32[]{:S(2)}) %collective-permute-start) | collective-permute-done | bytes 1048608 | tf_op jit(solution)/shard_map/ppermute | solution.py:18
  227.4 13.9 %all-reduce.4 = (f32[256]{0:T(256)S(1)}, f32[256]{0:T(256)S(1)}) all-reduce(f32[256]{0:T(256)S(1)} %get-tuple-element.87, f32[256]{0:T(256)S(1)} %get-tuple-element.86), channel_id=1, replica_groups=mesh['groups'=2,'section'=2,'shard'=8] {'shard'}, use_global_device_ids=true, to_apply=%region_21.22 | all-reduce | flops 512 | bytes 4096 | tf_op jit(solution)/shard_map/psum | solution.py:48
  250.5 54.8 %all-reduce.44.cloned.1.call-done = (f32[256,64]{0,1:T(8,128)}, f32[256,64]{0,1:T(8,128)}) async-done(((f32[256,64]{0,1:T(8,128)}, f32[256,64]{0,1:T(8,128)}), (f32[256,64]{0,1:T(8,128)}, f32[256,64]{0,1:T(8,128)})) %all-reduce.44.cloned.1.call-update) | async-done | bytes 131088 | tf_op jit(solution)/shard_map/psum | solution.py:55
  311.1 13.8 %all-reduce.3 = (f32[256]{0:T(256)S(1)}, f32[256]{0:T(256)S(1)}) all-reduce(f32[256]{0:T(256)S(1)} %get-tuple-element.85, f32[256]{0:T(256)S(1)} %get-tuple-element.84), channel_id=1, replica_groups=mesh['groups'=2,'section'=2,'shard'=8] {'shard'}, use_global_device_ids=true, to_apply=%region_30.31 | all-reduce | flops 512 | bytes 4096 | tf_op jit(solution)/shard_map/psum | solution.py:48
  335.0 53.5 %all-reduce.42.cloned.1.call-done = (f32[256,64]{0,1:T(8,128)}, f32[256,64]{0,1:T(8,128)}) async-done(((f32[256,64]{0,1:T(8,128)}, f32[256,64]{0,1:T(8,128)}), (f32[256,64]{0,1:T(8,128)}, f32[256,64]{0,1:T(8,128)})) %all-reduce.42.cloned.1.call-update) | async-done | bytes 131088 | tf_op jit(solution)/shard_map/psum | solution.py:55
  403.6 15.1 %collective-permute-done.3 = f32[256,1024]{1,0:T(8,128)S(1)} collective-permute-done((f32[256,1024]{1,0:T(8,128)S(1)}, f32[256,1024]{1,0:T(8,128)S(1)}, u32[]{:S(2)}, u32[]{:S(2)}) %collective-permute-start.3) | collective-permute-done | bytes 1048608 | tf_op jit(solution)/shard_map/ppermute | solution.py:18
  420.0 18.4 %collective-permute-done.2 = f32[256,1024]{1,0:T(8,128)S(1)} collective-permute-done((f32[256,1024]{1,0:T(8,128)S(1)}, f32[256,1024]{1,0:T(8,128)S(1)}, u32[]{:S(2)}, u32[]{:S(2)}) %collective-permute-start.2) | collective-permute-done | bytes 1048608 | tf_op jit(solution)/shard_map/ppermute | solution.py:18
  439.6 13.7 %all-reduce.2 = (f32[256]{0:T(256)S(1)}, f32[256]{0:T(256)S(1)}) all-reduce(f32[256]{0:T(256)S(1)} %get-tuple-element.83, f32[256]{0:T(256)S(1)} %get-tuple-element.82), channel_id=1, replica_groups=mesh['groups'=2,'section'=2,'shard'=8] {'shard'}, use_global_device_ids=true, to_apply=%region_39.40 | all-reduce | flops 512 | bytes 4096 | tf_op jit(solution)/shard_map/psum | solution.py:48
  463.7 53.8 %all-reduce.40.cloned.1.call-done = (f32[256,64]{0,1:T(8,128)}, f32[256,64]{0,1:T(8,128)}) async-done(((f32[256,64]{0,1:T(8,128)}, f32[256,64]{0,1:T(8,128)}), (f32[256,64]{0,1:T(8,128)}, f32[256,64]{0,1:T(8,128)})) %all-reduce.40.cloned.1.call-update) | async-done | bytes 131088 | tf_op jit(solution)/shard_map/psum | solution.py:55
  523.3 13.7 %all-reduce.1 = (f32[256]{0:T(256)S(1)}, f32[256]{0:T(256)S(1)}) all-reduce(f32[256]{0:T(256)S(1)} %get-tuple-element.81, f32[256]{0:T(256)S(1)} %get-tuple-element.80), channel_id=1, replica_groups=mesh['groups'=2,'section'=2,'shard'=8] {'shard'}, use_global_device_ids=true, to_apply=%region_48.49 | all-reduce | flops 512 | bytes 4096 | tf_op jit(solution)/shard_map/psum | solution.py:48
  554.4 53.3 %all-reduce.38.cloned.1.call-done = (f32[256,64]{0,1:T(8,128)}, f32[256,64]{0,1:T(8,128)}) async-done(((f32[256,64]{0,1:T(8,128)}, f32[256,64]{0,1:T(8,128)}), (f32[256,64]{0,1:T(8,128)}, f32[256,64]{0,1:T(8,128)})) %all-reduce.38.cloned.1.call-update) | async-done | bytes 131088 | tf_op jit(solution)/shard_map/psum | solution.py:55
  617.5 52.5 %all-reduce.26.cloned.1.call-done = f32[256,64]{0,1:T(8,128)} async-done(((f32[256,64]{0,1:T(8,128)}), f32[256,64]{0,1:T(8,128)}) %all-reduce.26.cloned.1.call-update) | async-done | bytes 65552 | tf_op jit(solution)/shard_map/psum | solution.py:79
  673.4 13.8 %psum.292 = f32[256]{0:T(256)S(1)} all-reduce(f32[256]{0:T(256)S(1)} %get-tuple-element.181), channel_id=1, replica_groups=mesh['groups'=2,'section'=2,'shard'=8] {'shard'}, use_global_device_ids=true, to_apply=%region_59.60 | all-reduce | flops 256 | bytes 2048 | tf_op jit(solution)/shard_map/psum | solution.py:83
  692.3 51.0 %all-reduce.28.cloned.1.call-done = f32[256,64]{0,1:T(8,128)} async-done(((f32[256,64]{0,1:T(8,128)}), f32[256,64]{0,1:T(8,128)}) %all-reduce.28.cloned.1.call-update) | async-done | bytes 65552 | tf_op jit(solution)/shard_map/psum | solution.py:79
  746.9 13.7 %psum.294 = f32[256]{0:T(256)S(1)} all-reduce(f32[256]{0:T(256)S(1)} %get-tuple-element.183), channel_id=1, replica_groups=mesh['groups'=2,'section'=2,'shard'=8] {'shard'}, use_global_device_ids=true, to_apply=%region_63.64 | all-reduce | flops 256 | bytes 2048 | tf_op jit(solution)/shard_map/psum | solution.py:83
  772.9 16.5 %collective-permute-done.4 = f32[256,1024]{1,0:T(8,128)S(1)} collective-permute-done((f32[256,1024]{1,0:T(8,128)S(1)}, f32[256,1024]{1,0:T(8,128)S(1)}, u32[]{:S(2)}, u32[]{:S(2)}) %collective-permute-start.4) | collective-permute-done | bytes 1048608 | tf_op jit(solution)/shard_map/ppermute | solution.py:18
  794.5 47.8 %all-reduce.30.cloned.1.call-done = f32[256,64]{0,1:T(8,128)} async-done(((f32[256,64]{0,1:T(8,128)}), f32[256,64]{0,1:T(8,128)}) %all-reduce.30.cloned.1.call-update) | async-done | bytes 65552 | tf_op jit(solution)/shard_map/psum | solution.py:79
  845.6 14.2 %psum.296 = f32[256]{0:T(256)S(1)} all-reduce(f32[256]{0:T(256)S(1)} %get-tuple-element.185), channel_id=1, replica_groups=mesh['groups'=2,'section'=2,'shard'=8] {'shard'}, use_global_device_ids=true, to_apply=%region_67.68 | all-reduce | flops 256 | bytes 2048 | tf_op jit(solution)/shard_map/psum | solution.py:83
  868.6 47.0 %all-reduce.32.cloned.1.call-done = f32[256,64]{0,1:T(8,128)} async-done(((f32[256,64]{0,1:T(8,128)}), f32[256,64]{0,1:T(8,128)}) %all-reduce.32.cloned.1.call-update) | async-done | bytes 65552 | tf_op jit(solution)/shard_map/psum | solution.py:79
  919.2 13.8 %psum.298 = f32[256]{0:T(256)S(1)} all-reduce(f32[256]{0:T(256)S(1)} %get-tuple-element.187), channel_id=1, replica_groups=mesh['groups'=2,'section'=2,'shard'=8] {'shard'}, use_global_device_ids=true, to_apply=%region_71.72 | all-reduce | flops 256 | bytes 2048 | tf_op jit(solution)/shard_map/psum | solution.py:83
  943.5 18.5 %collective-permute-done.5 = f32[256,1024]{1,0:T(8,128)S(1)} collective-permute-done((f32[256,1024]{1,0:T(8,128)S(1)}, f32[256,1024]{1,0:T(8,128)S(1)}, u32[]{:S(2)}, u32[]{:S(2)}) %collective-permute-start.5) | collective-permute-done | bytes 1048608 | tf_op jit(solution)/shard_map/ppermute | solution.py:18
  966.1 48.8 %all-reduce.34.cloned.1.call-done = f32[256,64]{0,1:T(8,128)} async-done(((f32[256,64]{0,1:T(8,128)}), f32[256,64]{0,1:T(8,128)}) %all-reduce.34.cloned.1.call-update) | async-done | bytes 65552 | tf_op jit(solution)/shard_map/psum | solution.py:79
  1018.2 13.7 %psum.300 = f32[256]{0:T(256)S(1)} all-reduce(f32[256]{0:T(256)S(1)} %get-tuple-element.189), channel_id=1, replica_groups=mesh['groups'=2,'section'=2,'shard'=8] {'shard'}, use_global_device_ids=true, to_apply=%region_75.76 | all-reduce | flops 256 | bytes 2048 | tf_op jit(solution)/shard_map/psum | solution.py:83
  1042.9 44.9 %all-reduce.36.cloned.1.call-done = f32[256,64]{0,1:T(8,128)} async-done(((f32[256,64]{0,1:T(8,128)}), f32[256,64]{0,1:T(8,128)}) %all-reduce.36.cloned.1.call-update) | async-done | bytes 65552 | tf_op jit(solution)/shard_map/psum | solution.py:79
  1097.2 31.2 %all-reduce = (f32[]{:T(128)}, f32[]{:T(128)}) all-reduce(f32[]{:T(128)} %multiply_reduce_fusion.2, f32[]{:T(128)} %multiply_reduce_fusion.1), channel_id=1, replica_groups=mesh['groups'=2,'section'=2,'shard'=8] {'section','shard'}, use_global_device_ids=true, to_apply=%region_1.0 | all-reduce | flops 2 | bytes 16 | tf_op jit(solution)/shard_map/psum | solution.py:93
  1129.7 9.5 multiply_reduce_fusion
  1139.3 30.3 %psum.303 = f32[]{:T(128)} all-reduce(f32[]{:T(128)} %get-tuple-element.116), channel_id=1, replica_groups=mesh['groups'=2,'section'=2,'shard'=8] {'section','shard'}, use_global_device_ids=true, to_apply=%region_81.82 | all-reduce | flops 1 | bytes 8 | tf_op jit(solution)/shard_map/psum | solution.py:165
  (360 shorter events, 246.2 us)
Async XLA Ops:
  7.2 89.6 %all-reduce.48.cloned.1.call-start = ((), (), s32[]{:S(2)}) async-start(), calls=%async_computation.11 | async-start | bytes 262144 | tf_op jit(solution)/shard_map/psum | solution.py:55
  16.9 25.1 %copy-start = (f32[1,4,2,64,1024]{4,3,1,2,0:T(8,128)}, f32[1,4,2,64,1024]{4,3,1,2,0:T(8,128)S(1)}, u32[]{:S(2)}) copy-start(f32[1,4,2,64,1024]{4,3,1,2,0:T(8,128)S(1)} %copy.39) | copy-start | bytes 6291460
  44.0 132.3 %all-reduce.46.cloned.1.call-start = ((), (), s32[]{:S(2)}) async-start(), calls=%async_computation.10 | async-start | bytes 262144 | tf_op jit(solution)/shard_map/psum | solution.py:55
  123.6 181.7 %all-reduce.44.cloned.1.call-start = ((), (), s32[]{:S(2)}) async-start(), calls=%async_computation.9 | async-start | bytes 262144 | tf_op jit(solution)/shard_map/psum | solution.py:55
  179.5 27.0 %collective-permute-start.1 = (f32[256,1024]{1,0:T(8,128)S(1)}, f32[256,1024]{1,0:T(8,128)S(1)}, u32[]{:S(2)}, u32[]{:S(2)}) collective-permute-start(f32[256,1024]{1,0:T(8,128)S(1)} %fusion.8), channel_id=1, source_target_pairs={{0,8},{1,9},{2,10},{3,11},{4,12},{5,13},{6,14},{7,15},{16,24},{17,... | collective-permute-start | bytes 3145736 | tf_op jit(solution)/shard_map/ppermute | solution.py:18
  184.4 41.7 %collective-permute-start = (f32[256,1024]{1,0:T(8,128)S(1)}, f32[256,1024]{1,0:T(8,128)S(1)}, u32[]{:S(2)}, u32[]{:S(2)}) collective-permute-start(f32[256,1024]{1,0:T(8,128)S(1)} %get-tuple-element.176), channel_id=1, source_target_pairs={{0,8},{1,9},{2,10},{3,11},{4,12},{5,13},{6,14},{7,15},{16,24},{17,... | collective-permute-start | bytes 3145736 | tf_op jit(solution)/shard_map/ppermute | solution.py:18
  185.8 20.7 %copy-start.19 = (f32[512,1024]{1,0:T(8,128)S(1)}, f32[512,1024]{1,0:T(8,128)}, u32[]{:S(2)}) copy-start(f32[512,1024]{1,0:T(8,128)} %convert_element_type.10) | copy-start | bytes 6291460
  250.3 138.2 %all-reduce.42.cloned.1.call-start = ((), (), s32[]{:S(2)}) async-start(), calls=%async_computation.8 | async-start | bytes 262144 | tf_op jit(solution)/shard_map/psum | solution.py:55
  311.1 17.3 %copy-start.24 = (f32[256,1024]{1,0:T(8,128)S(1)}, f32[256,1024]{1,0:T(8,128)}, u32[]{:S(2)}) copy-start(f32[256,1024]{1,0:T(8,128)} %get-tuple-element.177) | copy-start | bytes 3145732
  334.6 182.9 %all-reduce.40.cloned.1.call-start = ((), (), s32[]{:S(2)}) async-start(), calls=%async_computation.7 | async-start | bytes 262144 | tf_op jit(solution)/shard_map/psum | solution.py:55
  388.6 6.6 copy-start.34
  388.6 6.6 copy-start.46
  388.6 6.6 copy-start.74
  391.7 27.0 %collective-permute-start.3 = (f32[256,1024]{1,0:T(8,128)S(1)}, f32[256,1024]{1,0:T(8,128)S(1)}, u32[]{:S(2)}, u32[]{:S(2)}) collective-permute-start(f32[256,1024]{1,0:T(8,128)S(1)} %fusion.12), channel_id=1, source_target_pairs={{0,8},{1,9},{2,10},{3,11},{4,12},{5,13},{6,14},{7,15},{16,24},{17,... | collective-permute-start | bytes 3145736 | tf_op jit(solution)/shard_map/ppermute | solution.py:18
  397.8 40.6 %collective-permute-start.2 = (f32[256,1024]{1,0:T(8,128)S(1)}, f32[256,1024]{1,0:T(8,128)S(1)}, u32[]{:S(2)}, u32[]{:S(2)}) collective-permute-start(f32[256,1024]{1,0:T(8,128)S(1)} %get-tuple-element.179), channel_id=1, source_target_pairs={{0,8},{1,9},{2,10},{3,11},{4,12},{5,13},{6,14},{7,15},{16,24},{17,... | collective-permute-start | bytes 3145736 | tf_op jit(solution)/shard_map/ppermute | solution.py:18
  401.6 17.1 %copy-start.20 = (f32[512,1024]{1,0:T(8,128)S(1)}, f32[512,1024]{1,0:T(8,128)}, u32[]{:S(2)}) copy-start(f32[512,1024]{1,0:T(8,128)} %convert_element_type.10) | copy-start | bytes 6291460
  463.4 144.4 %all-reduce.38.cloned.1.call-start = ((), (), s32[]{:S(2)}) async-start(), calls=%async_computation.6 | async-start | bytes 262144 | tf_op jit(solution)/shard_map/psum | solution.py:55
  537.0 6.2 copy-start.29
  537.0 6.2 copy-start.60
  553.7 116.3 %all-reduce.26.cloned.1.call-start = ((), (), s32[]{:S(2)}) async-start(), calls=%async_computation | async-start | bytes 131072 | tf_op jit(solution)/shard_map/psum | solution.py:79
  617.2 126.0 %all-reduce.28.cloned.1.call-start = ((), (), s32[]{:S(2)}) async-start(), calls=%async_computation.1 | async-start | bytes 131072 | tf_op jit(solution)/shard_map/psum | solution.py:79
  691.4 150.9 %all-reduce.30.cloned.1.call-start = ((), (), s32[]{:S(2)}) async-start(), calls=%async_computation.2 | async-start | bytes 131072 | tf_op jit(solution)/shard_map/psum | solution.py:79
  762.6 26.8 %collective-permute-start.4 = (f32[256,1024]{1,0:T(8,128)S(1)}, f32[256,1024]{1,0:T(8,128)S(1)}, u32[]{:S(2)}, u32[]{:S(2)}) collective-permute-start(f32[256,1024]{1,0:T(8,128)S(1)} %fusion.105), channel_id=1, source_target_pairs={{8,0},{9,1},{10,2},{11,3},{12,4},{13,5},{14,6},{15,7},{24,16},{25,... | collective-permute-start | bytes 3145736 | tf_op jit(solution)/shard_map/ppermute | solution.py:18
  791.3 124.3 %all-reduce.32.cloned.1.call-start = ((), (), s32[]{:S(2)}) async-start(), calls=%async_computation.3 | async-start | bytes 131072 | tf_op jit(solution)/shard_map/psum | solution.py:79
  863.7 151.2 %all-reduce.34.cloned.1.call-start = ((), (), s32[]{:S(2)}) async-start(), calls=%async_computation.4 | async-start | bytes 131072 | tf_op jit(solution)/shard_map/psum | solution.py:79
  933.0 7.0 copy-start.50
  933.0 7.0 copy-start.54
  935.3 26.8 %collective-permute-start.5 = (f32[256,1024]{1,0:T(8,128)S(1)}, f32[256,1024]{1,0:T(8,128)S(1)}, u32[]{:S(2)}, u32[]{:S(2)}) collective-permute-start(f32[256,1024]{1,0:T(8,128)S(1)} %fusion.90), channel_id=1, source_target_pairs={{8,0},{9,1},{10,2},{11,3},{12,4},{13,5},{14,6},{15,7},{24,16},{25,... | collective-permute-start | bytes 3145736 | tf_op jit(solution)/shard_map/ppermute | solution.py:18
  942.8 19.3 %copy-start.32 = (f32[512,1024]{1,0:T(8,128)S(1)}, f32[512,1024]{1,0:T(8,128)}, u32[]{:S(2)}) copy-start(f32[512,1024]{1,0:T(8,128)} %copy-done.30) | copy-start | bytes 6291460
  943.5 19.7 %copy-start.11 = (f32[2,4,2,64,1024]{4,3,1,2,0:T(8,128)}, f32[2,4,2,64,1024]{4,3,1,2,0:T(8,128)S(1)}, u32[]{:S(2)}) copy-start(f32[2,4,2,64,1024]{4,3,1,2,0:T(8,128)S(1)} %fusion.2) | copy-start | bytes 12582916
  963.9 123.9 %all-reduce.36.cloned.1.call-start = ((), (), s32[]{:S(2)}) async-start(), calls=%async_computation.5 | async-start | bytes 131072 | tf_op jit(solution)/shard_map/psum | solution.py:79
  1041.9 46.0 %copy-start.23 = (f32[1,512,1024]{2,1,0:T(8,128)S(1)}, f32[1,512,1024]{2,1,0:T(8,128)}, u32[]{:S(2)}) copy-start(f32[1,512,1024]{2,1,0:T(8,128)} %get-tuple-element.124) | copy-start | bytes 6291460
  (68 other events, 192.0 us)
Sparse Core Ops, SparseCore 0:
  44.1 52.6 all-reduce.47
  123.7 52.5 all-reduce.45
  250.4 54.7 all-reduce.43
  334.7 53.8 all-reduce.41
  463.5 53.9 all-reduce.39
  553.9 53.8 all-reduce.37
  617.4 52.6 all-reduce.25
  691.5 51.7 all-reduce.27
  791.4 50.8 all-reduce.29
  863.8 51.7 all-reduce.31
  964.0 50.8 all-reduce.33
  1036.0 51.7 all-reduce.35
where the time goes:
time: 1210 us; the launch traced here: 1200 us
  waiting for transfers between devices  707 us (58%)
  blocking collectives  218 us (18%)
  matrix products  109 us (9%)
  other arithmetic  80.2 us (7%)
  local copies, waits for them, and re-layouts  52.5 us (4%)
  between operations  18.5 us (2%)
  starting transfers between devices  13.9 us (1%)
    psum x6, waiting for transfers between devices, layer_forward(): lax.psum((pick_down(normed, parameters[:, 0], onehot) * down_scale, (pick...  310 us
    psum x6, waiting for transfers between devices, layer_backward(): low_cot = lax.psum(partial_cot, 'shard')  292 us
    ppermute x6, waiting for transfers between devices, shifted(): lax.ppermute(value, axis, [(source, source + steps) for source in range(i...  104 us
    psum x6, blocking collectives, layer_forward(): lax.psum((jnp.sum(hidden * hidden, axis=-1), jnp.sum(hidden * moving, axi...  87.1 us
    psum x5, blocking collectives, layer_backward(): lax.psum(jnp.sum(cot_norm * gain_vector * hidden, axis=-1), 'shard')  69.1 us
    dot_general x22, matrix products, apply_up_projection(): return jnp.einsum('tkr,krd->td', picked, mats, precision=HIGH)  48.2 us
    dot_general x24, matrix products, pick_down(): expanded = jnp.einsum('td,krd->tkr', values, mats, precision=HIGH)  42.6 us
    psum x1, blocking collectives, body(): squared_old = lax.psum(jnp.sum(residual * residual), ('section', 'shard'))  31.2 us
  transfers between devices with their start and end apart: 18, of which 18 were waited for; matrix products, arithmetic and copies ran while one was open for 5% of the time, Pallas kernels for 0%

commit v1 on v0

--- a/solution.py
+++ b/solution.py
@@ -76,7 +76,7 @@
     up_projection_scale = ADAPTER_SCALE * ADAPTER_RANK ** (-0.5)
     grad_up = up_projection_scale * task_outer(lowrank, cotangent, onehot)
     partial_cot = up_projection_scale * pick_down(cotangent, parameters[:, 1], onehot)
-    low_cot = lax.psum(partial_cot, "shard")
+    low_cot = jnp.sum(lax.all_gather(partial_cot, "shard"), axis=0)
     normed = hidden * gain_vector * recip[:, None]
     grad_down = down_scale * task_outer(low_cot, normed, onehot)
     cot_norm = down_scale * apply_up_projection(low_cot, parameters[:, 0], onehot)

time: 1210 us -> 984 us (0.81)
  waiting for transfers between devices: 707 us -> 414 us
  blocking collectives: 218 us -> 310 us
  other arithmetic: 80.2 us -> 63.5 us
    psum x6 -> x0, waiting for transfers between devices: 292 us -> none  [layer_backward(): low_cot = lax.psum(partial_cot, 'shard')]
    all_gather x0 -> x6, blocking collectives: none -> 90.3 us  [layer_backward(): low_cot = jnp.sum(lax.all_gather(partial_cot, 'shard'), axis=0)]
    unnamed x170 -> x204, local copies, waits for them, and re-layouts: 23.6 us -> 24.6 us
  transfers between devices with their start and end apart: 18 -> 12, of which waited for: 18 -> 12; matrix products, arithmetic and copies ran while one was open for 5% -> 4% of each run, Pallas kernels for 0% -> 0%
where the time goes in v1:
time: 984 us; the launch traced here: 975 us
  waiting for transfers between devices  414 us (42%)
  blocking collectives  310 us (32%)
  matrix products  99 us (10%)
  other arithmetic  63.5 us (6%)
  local copies, waits for them, and re-layouts  56 us (6%)
  between operations  18.8 us (2%)
  starting transfers between devices  13.5 us (1%)
    psum x6, waiting for transfers between devices, layer_forward(): lax.psum((pick_down(normed, parameters[:, 0], onehot) * down_scale, (pick...  309 us
    ppermute x6, waiting for transfers between devices, shifted(): lax.ppermute(value, axis, [(source, source + steps) for source in range(i...  105 us
    all_gather x6, blocking collectives, layer_backward(): low_cot = jnp.sum(lax.all_gather(partial_cot, 'shard'), axis=0)  90.3 us
    psum x6, blocking collectives, layer_forward(): lax.psum((jnp.sum(hidden * hidden, axis=-1), jnp.sum(hidden * moving, axi...  87.5 us
    psum x5, blocking collectives, layer_backward(): lax.psum(jnp.sum(cot_norm * gain_vector * hidden, axis=-1), 'shard')  71.6 us
    dot_general x24, matrix products, pick_down(): expanded = jnp.einsum('td,krd->tkr', values, mats, precision=HIGH)  42.5 us
    dot_general x22, matrix products, apply_up_projection(): return jnp.einsum('tkr,krd->td', picked, mats, precision=HIGH)  42 us
    psum x1, blocking collectives, body(): squared_old = lax.psum(jnp.sum(residual * residual), ('section', 'shard'))  30.4 us
  transfers between devices with their start and end apart: 12, of which 12 were waited for; matrix products, arithmetic and copies ran while one was open for 4% of the time, Pallas kernels for 0%

profile of v1, /device:TPU:0, one launch (start us, length us, event | category | flops | bytes accessed | tf_op | source)
XLA Modules:
  0.0 974.9 jit_solution(11028555463367784960)
XLA Ops:
  19.2 18.1 %all-reduce.6 = (f32[256]{0:T(256)S(1)}, f32[256]{0:T(256)S(1)}) all-reduce(f32[256]{0:T(256)S(1)} %get-tuple-element.82, f32[256]{0:T(256)S(1)} %get-tuple-element.81), channel_id=1, replica_groups=mesh['groups'=2,'section'=2,'shard'=8] {'shard'}, use_global_device_ids=true, to_apply=%region_3.4 | all-reduce | flops 512 | bytes 4096 | tf_op jit(solution)/shard_map/psum | solution.py:48
  56.0 41.2 %all-reduce.30.cloned.1.call-done = (f32[256,64]{0,1:T(8,128)}, f32[256,64]{0,1:T(8,128)}) async-done(((f32[256,64]{0,1:T(8,128)}, f32[256,64]{0,1:T(8,128)}), (f32[256,64]{0,1:T(8,128)}, f32[256,64]{0,1:T(8,128)})) %all-reduce.30.cloned.1.call-update) | async-done | bytes 131088 | tf_op jit(solution)/shard_map/psum | solution.py:55
  102.6 14.2 %all-reduce.5 = (f32[256]{0:T(256)S(1)}, f32[256]{0:T(256)S(1)}) all-reduce(f32[256]{0:T(256)S(1)} %get-tuple-element.92, f32[256]{0:T(256)S(1)} %get-tuple-element.91), channel_id=1, replica_groups=mesh['groups'=2,'section'=2,'shard'=8] {'shard'}, use_global_device_ids=true, to_apply=%region_12.13 | all-reduce | flops 512 | bytes 4096 | tf_op jit(solution)/shard_map/psum | solution.py:48
  124.6 52.4 %all-reduce.28.cloned.1.call-done = (f32[256,64]{0,1:T(8,128)}, f32[256,64]{0,1:T(8,128)}) async-done(((f32[256,64]{0,1:T(8,128)}, f32[256,64]{0,1:T(8,128)}), (f32[256,64]{0,1:T(8,128)}, f32[256,64]{0,1:T(8,128)})) %all-reduce.28.cloned.1.call-update) | async-done | bytes 131088 | tf_op jit(solution)/shard_map/psum | solution.py:55
  189.8 17.4 %collective-permute-done.1 = f32[256,1024]{1,0:T(8,128)S(1)} collective-permute-done((f32[256,1024]{1,0:T(8,128)S(1)}, f32[256,1024]{1,0:T(8,128)S(1)}, u32[]{:S(2)}, u32[]{:S(2)}) %collective-permute-start.1) | collective-permute-done | bytes 1048608 | tf_op jit(solution)/shard_map/ppermute | solution.py:18
  208.4 18.4 %collective-permute-done = f32[256,1024]{1,0:T(8,128)S(1)} collective-permute-done((f32[256,1024]{1,0:T(8,128)S(1)}, f32[256,1024]{1,0:T(8,128)S(1)}, u32[]{:S(2)}, u32[]{:S(2)}) %collective-permute-start) | collective-permute-done | bytes 1048608 | tf_op jit(solution)/shard_map/ppermute | solution.py:18
  228.2 13.9 %all-reduce.4 = (f32[256]{0:T(256)S(1)}, f32[256]{0:T(256)S(1)}) all-reduce(f32[256]{0:T(256)S(1)} %get-tuple-element.90, f32[256]{0:T(256)S(1)} %get-tuple-element.89), channel_id=1, replica_groups=mesh['groups'=2,'section'=2,'shard'=8] {'shard'}, use_global_device_ids=true, to_apply=%region_21.22 | all-reduce | flops 512 | bytes 4096 | tf_op jit(solution)/shard_map/psum | solution.py:48
  251.1 54.8 %all-reduce.26.cloned.1.call-done = (f32[256,64]{0,1:T(8,128)}, f32[256,64]{0,1:T(8,128)}) async-done(((f32[256,64]{0,1:T(8,128)}, f32[256,64]{0,1:T(8,128)}), (f32[256,64]{0,1:T(8,128)}, f32[256,64]{0,1:T(8,128)})) %all-reduce.26.cloned.1.call-update) | async-done | bytes 131088 | tf_op jit(solution)/shard_map/psum | solution.py:55
  311.8 13.8 %all-reduce.3 = (f32[256]{0:T(256)S(1)}, f32[256]{0:T(256)S(1)}) all-reduce(f32[256]{0:T(256)S(1)} %get-tuple-element.88, f32[256]{0:T(256)S(1)} %get-tuple-element.87), channel_id=1, replica_groups=mesh['groups'=2,'section'=2,'shard'=8] {'shard'}, use_global_device_ids=true, to_apply=%region_30.31 | all-reduce | flops 512 | bytes 4096 | tf_op jit(solution)/shard_map/psum | solution.py:48
  335.6 53.7 %all-reduce.24.cloned.1.call-done = (f32[256,64]{0,1:T(8,128)}, f32[256,64]{0,1:T(8,128)}) async-done(((f32[256,64]{0,1:T(8,128)}, f32[256,64]{0,1:T(8,128)}), (f32[256,64]{0,1:T(8,128)}, f32[256,64]{0,1:T(8,128)})) %all-reduce.24.cloned.1.call-update) | async-done | bytes 131088 | tf_op jit(solution)/shard_map/psum | solution.py:55
  404.3 15.1 %collective-permute-done.3 = f32[256,1024]{1,0:T(8,128)S(1)} collective-permute-done((f32[256,1024]{1,0:T(8,128)S(1)}, f32[256,1024]{1,0:T(8,128)S(1)}, u32[]{:S(2)}, u32[]{:S(2)}) %collective-permute-start.3) | collective-permute-done | bytes 1048608 | tf_op jit(solution)/shard_map/ppermute | solution.py:18
  420.7 18.4 %collective-permute-done.2 = f32[256,1024]{1,0:T(8,128)S(1)} collective-permute-done((f32[256,1024]{1,0:T(8,128)S(1)}, f32[256,1024]{1,0:T(8,128)S(1)}, u32[]{:S(2)}, u32[]{:S(2)}) %collective-permute-start.2) | collective-permute-done | bytes 1048608 | tf_op jit(solution)/shard_map/ppermute | solution.py:18
  440.3 13.7 %all-reduce.2 = (f32[256]{0:T(256)S(1)}, f32[256]{0:T(256)S(1)}) all-reduce(f32[256]{0:T(256)S(1)} %get-tuple-element.86, f32[256]{0:T(256)S(1)} %get-tuple-element.85), channel_id=1, replica_groups=mesh['groups'=2,'section'=2,'shard'=8] {'shard'}, use_global_device_ids=true, to_apply=%region_39.40 | all-reduce | flops 512 | bytes 4096 | tf_op jit(solution)/shard_map/psum | solution.py:48
  464.7 53.5 %all-reduce.22.cloned.1.call-done = (f32[256,64]{0,1:T(8,128)}, f32[256,64]{0,1:T(8,128)}) async-done(((f32[256,64]{0,1:T(8,128)}, f32[256,64]{0,1:T(8,128)}), (f32[256,64]{0,1:T(8,128)}, f32[256,64]{0,1:T(8,128)})) %all-reduce.22.cloned.1.call-update) | async-done | bytes 131088 | tf_op jit(solution)/shard_map/psum | solution.py:55
  524.0 13.7 %all-reduce.1 = (f32[256]{0:T(256)S(1)}, f32[256]{0:T(256)S(1)}) all-reduce(f32[256]{0:T(256)S(1)} %get-tuple-element.84, f32[256]{0:T(256)S(1)} %get-tuple-element.83), channel_id=1, replica_groups=mesh['groups'=2,'section'=2,'shard'=8] {'shard'}, use_global_device_ids=true, to_apply=%region_48.49 | all-reduce | flops 512 | bytes 4096 | tf_op jit(solution)/shard_map/psum | solution.py:48
  555.7 53.4 %all-reduce.20.cloned.1.call-done = (f32[256,64]{0,1:T(8,128)}, f32[256,64]{0,1:T(8,128)}) async-done(((f32[256,64]{0,1:T(8,128)}, f32[256,64]{0,1:T(8,128)}), (f32[256,64]{0,1:T(8,128)}, f32[256,64]{0,1:T(8,128)})) %all-reduce.20.cloned.1.call-update) | async-done | bytes 131088 | tf_op jit(solution)/shard_map/psum | solution.py:55
  616.6 15.2 %all-gather = f32[2048,64]{0,1:T(8,128)S(1)} all-gather(f32[256,64]{0,1:T(8,128)S(1)} %broadcast_multiply_fusion.6), channel_id=2, replica_groups=mesh['groups'=2,'section'=2,'shard'=8] {'shard'}, dimensions={0}, use_global_device_ids=true | all-gather | bytes 589824 | tf_op jit(solution)/shard_map/all_gather | solution.py:79
  634.2 15.0 %psum.249 = f32[256]{0:T(256)S(1)} all-reduce(f32[256]{0:T(256)S(1)} %get-tuple-element.184), channel_id=1, replica_groups=mesh['groups'=2,'section'=2,'shard'=8] {'shard'}, use_global_device_ids=true, to_apply=%region_59.60 | all-reduce | flops 256 | bytes 2048 | tf_op jit(solution)/shard_map/psum | solution.py:83
  652.9 15.0 %all-gather.1 = f32[2048,64]{0,1:T(8,128)S(1)} all-gather(f32[256,64]{0,1:T(8,128)S(1)} %broadcast_multiply_fusion.5), channel_id=3, replica_groups=mesh['groups'=2,'section'=2,'shard'=8] {'shard'}, dimensions={0}, use_global_device_ids=true | all-gather | bytes 589824 | tf_op jit(solution)/shard_map/all_gather | solution.py:79
  670.9 14.6 %psum.250 = f32[256]{0:T(256)} all-reduce(f32[256]{0:T(256)} %get-tuple-element.186), channel_id=1, replica_groups=mesh['groups'=2,'section'=2,'shard'=8] {'shard'}, use_global_device_ids=true, to_apply=%region_63.64 | all-reduce | flops 256 | bytes 2048 | tf_op jit(solution)/shard_map/psum | solution.py:83
  698.4 16.4 %collective-permute-done.4 = f32[256,1024]{1,0:T(8,128)S(1)} collective-permute-done((f32[256,1024]{1,0:T(8,128)S(1)}, f32[256,1024]{1,0:T(8,128)S(1)}, u32[]{:S(2)}, u32[]{:S(2)}) %collective-permute-start.4) | collective-permute-done | bytes 1048608 | tf_op jit(solution)/shard_map/ppermute | solution.py:18
  716.0 14.9 %all-gather.2 = f32[2048,64]{0,1:T(8,128)S(1)} all-gather(f32[256,64]{0,1:T(8,128)S(1)} %broadcast_multiply_fusion.4), channel_id=4, replica_groups=mesh['groups'=2,'section'=2,'shard'=8] {'shard'}, dimensions={0}, use_global_device_ids=true | all-gather | bytes 589824 | tf_op jit(solution)/shard_map/all_gather | solution.py:79
  733.3 14.0 %psum.251 = f32[256]{0:T(256)S(1)} all-reduce(f32[256]{0:T(256)S(1)} %get-tuple-element.188), channel_id=1, replica_groups=mesh['groups'=2,'section'=2,'shard'=8] {'shard'}, use_global_device_ids=true, to_apply=%region_67.68 | all-reduce | flops 256 | bytes 2048 | tf_op jit(solution)/shard_map/psum | solution.py:83
  750.5 15.4 %all-gather.3 = f32[2048,64]{0,1:T(8,128)S(1)} all-gather(f32[256,64]{0,1:T(8,128)S(1)} %broadcast_multiply_fusion.3), channel_id=5, replica_groups=mesh['groups'=2,'section'=2,'shard'=8] {'shard'}, dimensions={0}, use_global_device_ids=true | all-gather | bytes 589824 | tf_op jit(solution)/shard_map/all_gather | solution.py:79
  768.4 13.9 %psum.252 = f32[256]{0:T(256)S(1)} all-reduce(f32[256]{0:T(256)S(1)} %get-tuple-element.190), channel_id=1, replica_groups=mesh['groups'=2,'section'=2,'shard'=8] {'shard'}, use_global_device_ids=true, to_apply=%region_71.72 | all-reduce | flops 256 | bytes 2048 | tf_op jit(solution)/shard_map/psum | solution.py:83
  792.3 19.2 %collective-permute-done.5 = f32[256,1024]{1,0:T(8,128)S(1)} collective-permute-done((f32[256,1024]{1,0:T(8,128)S(1)}, f32[256,1024]{1,0:T(8,128)S(1)}, u32[]{:S(2)}, u32[]{:S(2)}) %collective-permute-start.5) | collective-permute-done | bytes 1048608 | tf_op jit(solution)/shard_map/ppermute | solution.py:18
  812.6 14.9 %all-gather.4 = f32[2048,64]{0,1:T(8,128)S(1)} all-gather(f32[256,64]{0,1:T(8,128)S(1)} %broadcast_multiply_fusion.2), channel_id=6, replica_groups=mesh['groups'=2,'section'=2,'shard'=8] {'shard'}, dimensions={0}, use_global_device_ids=true | all-gather | bytes 589824 | tf_op jit(solution)/shard_map/all_gather | solution.py:79
  829.9 14.1 %psum.253 = f32[256]{0:T(256)S(1)} all-reduce(f32[256]{0:T(256)S(1)} %get-tuple-element.192), channel_id=1, replica_groups=mesh['groups'=2,'section'=2,'shard'=8] {'shard'}, use_global_device_ids=true, to_apply=%region_75.76 | all-reduce | flops 256 | bytes 2048 | tf_op jit(solution)/shard_map/psum | solution.py:83
  849.5 15.0 %all-gather.5 = f32[2048,64]{0,1:T(8,128)S(1)} all-gather(f32[256,64]{0,1:T(8,128)S(1)} %broadcast_multiply_fusion.1), channel_id=7, replica_groups=mesh['groups'=2,'section'=2,'shard'=8] {'shard'}, dimensions={0}, use_global_device_ids=true | all-gather | bytes 589824 | tf_op jit(solution)/shard_map/all_gather | solution.py:79
  874.3 30.4 %all-reduce = (f32[]{:T(128)}, f32[]{:T(128)}) all-reduce(f32[]{:T(128)} %multiply_reduce_fusion.2, f32[]{:T(128)} %multiply_reduce_fusion.1), channel_id=1, replica_groups=mesh['groups'=2,'section'=2,'shard'=8] {'section','shard'}, use_global_device_ids=true, to_apply=%region_1.0 | all-reduce | flops 2 | bytes 16 | tf_op jit(solution)/shard_map/psum | solution.py:93
  906.1 9.5 multiply_reduce_fusion
  915.6 30.3 %psum.255 = f32[]{:T(128)} all-reduce(f32[]{:T(128)} %get-tuple-element.119), channel_id=1, replica_groups=mesh['groups'=2,'section'=2,'shard'=8] {'section','shard'}, use_global_device_ids=true, to_apply=%region_81.82 | all-reduce | flops 1 | bytes 8 | tf_op jit(solution)/shard_map/psum | solution.py:165
  (388 shorter events, 222.6 us)
Async XLA Ops:
  7.2 90.0 %all-reduce.30.cloned.1.call-start = ((), (), s32[]{:S(2)}) async-start(), calls=%async_computation.5 | async-start | bytes 262144 | tf_op jit(solution)/shard_map/psum | solution.py:55
  16.9 25.6 %copy-start = (f32[1,4,2,64,1024]{4,3,1,2,0:T(8,128)}, f32[1,4,2,64,1024]{4,3,1,2,0:T(8,128)S(1)}, u32[]{:S(2)}) copy-start(f32[1,4,2,64,1024]{4,3,1,2,0:T(8,128)S(1)} %copy.58) | copy-start | bytes 6291460
  44.5 132.6 %all-reduce.28.cloned.1.call-start = ((), (), s32[]{:S(2)}) async-start(), calls=%async_computation.4 | async-start | bytes 262144 | tf_op jit(solution)/shard_map/psum | solution.py:55
  124.3 181.7 %all-reduce.26.cloned.1.call-start = ((), (), s32[]{:S(2)}) async-start(), calls=%async_computation.3 | async-start | bytes 262144 | tf_op jit(solution)/shard_map/psum | solution.py:55
  180.2 27.0 %collective-permute-start.1 = (f32[256,1024]{1,0:T(8,128)S(1)}, f32[256,1024]{1,0:T(8,128)S(1)}, u32[]{:S(2)}, u32[]{:S(2)}) collective-permute-start(f32[256,1024]{1,0:T(8,128)S(1)} %fusion.8), channel_id=1, source_target_pairs={{0,8},{1,9},{2,10},{3,11},{4,12},{5,13},{6,14},{7,15},{16,24},{17,... | collective-permute-start | bytes 3145736 | tf_op jit(solution)/shard_map/ppermute | solution.py:18
  185.1 41.7 %collective-permute-start = (f32[256,1024]{1,0:T(8,128)S(1)}, f32[256,1024]{1,0:T(8,128)S(1)}, u32[]{:S(2)}, u32[]{:S(2)}) collective-permute-start(f32[256,1024]{1,0:T(8,128)S(1)} %get-tuple-element.179), channel_id=1, source_target_pairs={{0,8},{1,9},{2,10},{3,11},{4,12},{5,13},{6,14},{7,15},{16,24},{17,... | collective-permute-start | bytes 3145736 | tf_op jit(solution)/shard_map/ppermute | solution.py:18
  186.5 20.7 %copy-start.22 = (f32[512,1024]{1,0:T(8,128)S(1)}, f32[512,1024]{1,0:T(8,128)}, u32[]{:S(2)}) copy-start(f32[512,1024]{1,0:T(8,128)} %convert_element_type.10) | copy-start | bytes 6291460
  251.0 138.3 %all-reduce.24.cloned.1.call-start = ((), (), s32[]{:S(2)}) async-start(), calls=%async_computation.2 | async-start | bytes 262144 | tf_op jit(solution)/shard_map/psum | solution.py:55
  311.8 17.3 %copy-start.29 = (f32[256,1024]{1,0:T(8,128)S(1)}, f32[256,1024]{1,0:T(8,128)}, u32[]{:S(2)}) copy-start(f32[256,1024]{1,0:T(8,128)} %get-tuple-element.180) | copy-start | bytes 3145732
  335.3 182.8 %all-reduce.22.cloned.1.call-start = ((), (), s32[]{:S(2)}) async-start(), calls=%async_computation.1 | async-start | bytes 262144 | tf_op jit(solution)/shard_map/psum | solution.py:55
  392.5 27.0 %collective-permute-start.3 = (f32[256,1024]{1,0:T(8,128)S(1)}, f32[256,1024]{1,0:T(8,128)S(1)}, u32[]{:S(2)}, u32[]{:S(2)}) collective-permute-start(f32[256,1024]{1,0:T(8,128)S(1)} %fusion.12), channel_id=1, source_target_pairs={{0,8},{1,9},{2,10},{3,11},{4,12},{5,13},{6,14},{7,15},{16,24},{17,... | collective-permute-start | bytes 3145736 | tf_op jit(solution)/shard_map/ppermute | solution.py:18
  398.5 40.6 %collective-permute-start.2 = (f32[256,1024]{1,0:T(8,128)S(1)}, f32[256,1024]{1,0:T(8,128)S(1)}, u32[]{:S(2)}, u32[]{:S(2)}) collective-permute-start(f32[256,1024]{1,0:T(8,128)S(1)} %get-tuple-element.182), channel_id=1, source_target_pairs={{0,8},{1,9},{2,10},{3,11},{4,12},{5,13},{6,14},{7,15},{16,24},{17,... | collective-permute-start | bytes 3145736 | tf_op jit(solution)/shard_map/ppermute | solution.py:18
  402.3 17.1 %copy-start.23 = (f32[512,1024]{1,0:T(8,128)S(1)}, f32[512,1024]{1,0:T(8,128)}, u32[]{:S(2)}) copy-start(f32[512,1024]{1,0:T(8,128)} %convert_element_type.10) | copy-start | bytes 6291460
  464.1 145.0 %all-reduce.20.cloned.1.call-start = ((), (), s32[]{:S(2)}) async-start(), calls=%async_computation | async-start | bytes 262144 | tf_op jit(solution)/shard_map/psum | solution.py:55
  615.5 16.6 %copy-start.35 = (f32[512,1024]{1,0:T(8,128)}, f32[512,1024]{1,0:T(8,128)S(1)}, u32[]{:S(2)}) copy-start(f32[512,1024]{1,0:T(8,128)S(1)} %broadcast_multiply_fusion) | copy-start | bytes 6291460
  615.5 16.6 %copy-start.16 = (f32[1,512,1024]{2,1,0:T(8,128)S(1)}, f32[1,512,1024]{2,1,0:T(8,128)}, u32[]{:S(2)}) copy-start(f32[1,512,1024]{2,1,0:T(8,128)} %get-tuple-element.128) | copy-start | bytes 6291460
  615.5 16.6 %copy-start.79 = (f32[1024]{0:T(1024)S(1)}, f32[1024]{0:T(1024)}, u32[]{:S(2)}) copy-start(f32[1024]{0:T(1024)} %broadcast_multiply_fusion.14) | copy-start | bytes 12292
  632.0 17.3 %copy-start.86 = (f32[1,256]{1,0:T(1,128)S(1)}, f32[1,256]{1,0:T(1,128)}, u32[]{:S(2)}) copy-start(f32[1,256]{1,0:T(1,128)} %get-tuple-element.194) | copy-start | bytes 3076
  651.8 16.4 %copy-start.24 = (f32[1,512,1024]{2,1,0:T(8,128)S(1)}, f32[1,512,1024]{2,1,0:T(8,128)}, u32[]{:S(2)}) copy-start(f32[1,512,1024]{2,1,0:T(8,128)} %get-tuple-element.127) | copy-start | bytes 6291460
  651.8 16.4 %copy-start.84 = (f32[1024]{0:T(1024)S(1)}, f32[1024]{0:T(1024)}, u32[]{:S(2)}) copy-start(f32[1024]{0:T(1024)} %broadcast_multiply_fusion.13) | copy-start | bytes 12292
  688.1 26.6 %collective-permute-start.4 = (f32[256,1024]{1,0:T(8,128)S(1)}, f32[256,1024]{1,0:T(8,128)S(1)}, u32[]{:S(2)}, u32[]{:S(2)}) collective-permute-start(f32[256,1024]{1,0:T(8,128)S(1)} %fusion.105), channel_id=1, source_target_pairs={{8,0},{9,1},{10,2},{11,3},{12,4},{13,5},{14,6},{15,7},{24,16},{25,... | collective-permute-start | bytes 3145736 | tf_op jit(solution)/shard_map/ppermute | solution.py:18
  714.9 16.2 %copy-start.80 = (f32[1024]{0:T(1024)S(1)}, f32[1024]{0:T(1024)}, u32[]{:S(2)}) copy-start(f32[1024]{0:T(1024)} %broadcast_multiply_fusion.14) | copy-start | bytes 12292
  749.4 16.8 %copy-start.52 = (f32[256,1024]{1,0:T(8,128)}, f32[256,1024]{1,0:T(8,128)S(1)}, u32[]{:S(2)}) copy-start(f32[256,1024]{1,0:T(8,128)S(1)} %fusion.97) | copy-start | bytes 3145732
  749.4 16.8 %copy-start.26 = (f32[1,512,1024]{2,1,0:T(8,128)S(1)}, f32[1,512,1024]{2,1,0:T(8,128)}, u32[]{:S(2)}) copy-start(f32[1,512,1024]{2,1,0:T(8,128)} %get-tuple-element.127) | copy-start | bytes 6291460
  749.4 16.8 %copy-start.85 = (f32[1024]{0:T(1024)S(1)}, f32[1024]{0:T(1024)}, u32[]{:S(2)}) copy-start(f32[1024]{0:T(1024)} %broadcast_multiply_fusion.13) | copy-start | bytes 12292
  766.1 16.3 %copy-start.90 = (f32[1,256]{1,0:T(1,128)S(1)}, f32[1,256]{1,0:T(1,128)}, u32[]{:S(2)}) copy-start(f32[1,256]{1,0:T(1,128)} %get-tuple-element.152) | copy-start | bytes 3076
  784.7 26.7 %collective-permute-start.5 = (f32[256,1024]{1,0:T(8,128)S(1)}, f32[256,1024]{1,0:T(8,128)S(1)}, u32[]{:S(2)}, u32[]{:S(2)}) collective-permute-start(f32[256,1024]{1,0:T(8,128)S(1)} %fusion.90), channel_id=1, source_target_pairs={{8,0},{9,1},{10,2},{11,3},{12,4},{13,5},{14,6},{15,7},{24,16},{25,... | collective-permute-start | bytes 3145736 | tf_op jit(solution)/shard_map/ppermute | solution.py:18
  791.5 19.9 %copy-start.37 = (f32[512,1024]{1,0:T(8,128)S(1)}, f32[512,1024]{1,0:T(8,128)}, u32[]{:S(2)}) copy-start(f32[512,1024]{1,0:T(8,128)} %copy-done.35) | copy-start | bytes 6291460
  792.2 37.7 %copy-start.11 = (f32[2,4,2,64,1024]{4,3,1,2,0:T(8,128)}, f32[2,4,2,64,1024]{4,3,1,2,0:T(8,128)S(1)}, u32[]{:S(2)}) copy-start(f32[2,4,2,64,1024]{4,3,1,2,0:T(8,128)S(1)} %fusion.2) | copy-start | bytes 12582916
  792.2 19.3 %copy-start.70 = (f32[256,4]{0,1:T(4,128)S(1)}, f32[256,4]{0,1:T(4,128)}, u32[]{:S(2)}) copy-start(f32[256,4]{0,1:T(4,128)} %get-tuple-element.141) | copy-start | bytes 12292
  827.7 16.4 %copy-start.88 = (f32[1,256]{1,0:T(1,128)S(1)}, f32[1,256]{1,0:T(1,128)}, u32[]{:S(2)}) copy-start(f32[1,256]{1,0:T(1,128)} %get-tuple-element.196) | copy-start | bytes 3076
  848.4 16.4 %copy-start.73 = (f32[256,64]{0,1:T(8,128)S(1)}, f32[256,64]{0,1:T(8,128)}, u32[]{:S(2)}) copy-start(f32[256,64]{0,1:T(8,128)} %get-tuple-element.135) | copy-start | bytes 196612
  (76 other events, 262.9 us)
Sparse Core Ops, SparseCore 0:
  44.6 52.5 all-reduce.29
  124.4 52.5 all-reduce.27
  251.1 54.7 all-reduce.25
  335.4 53.8 all-reduce.23
  464.2 53.8 all-reduce.21
  555.2 53.8 all-reduce.19
